TPU v7x, 512 devices: a whole 4x4x16 slice. The times are simulated.
512 devices in a mesh: req: 128 (over x, z, core), tp: 4 (over y).
Axes of the slice: x: 4, y: 4, z: 16, core: 2. Of those that a mesh axis runs over, the one named last changes fastest.
Arguments:
- queries: bfloat16 [2, 128, 32, 1536], P(None, 'req', None, 'tp')
- response_kv: bfloat16 [2, 128, 2, 32, 256], P(None, 'req'), may hold values from -6 to 6
- cache_kv: bfloat16 [2, 128, 2, 384, 256], P(None, 'req'), may hold values from -6 to 6
- residual: bfloat16 [2, 128, 32, 1536], P(None, 'req')
- out_proj: bfloat16 [2, 1536, 1536], P(None, 'tp'), may hold values from -0.5 to 0.5
- norm_gain: float32 [2, 1536], replicated, may hold values from 0.25 to 1.75
- lm_head: bfloat16 [2, 131072, 1536], P(None, 'req', 'tp')
- targets: int32 [128, 32], P(None, 'tp'), may hold values from 0 to 131071
- resp_lengths: int32 [128], replicated, may hold values from 1 to 32, 2560 in all
- cache_lengths: int32 [128], P('req'), may hold values from 1 to 384, 30720 in all
- owner_slot: int32 [128], replicated, may hold values from 0 to 127, each once
- sink_count: int32 [1], replicated, may hold values from 1 to 95
- window_size: int32 [1], replicated, may hold values from 48 to 191
Outputs:
- token_logprobs: float32 [128, 32], P('req', 'tp')
- request_scores: float32 [128, 2], P('req')
Inputs may be any that keep to these rules, and one draw needn't show every extreme that they name: `resp_lengths`: live response slots are the first ones; all lengths sum to 2560. `cache_lengths`: live cache slots are the first ones; all lengths sum to 30720. `owner_slot`: A permutation of the requests.
All inputs are finite; a program needn't handle non-finite values. No bound on the sum of `cache_lengths` on one device may be relied on, other than what follows from the above.
Results may differ from a plain program's by a relative error of at most 0.0014.
Values may be sent and summed in bfloat16 or wider, within the bound.
A program may use at most 128 MiB of HBM per device.

v0:
```python
import jax
import jax.numpy as jnp
from jax import lax
from jax.sharding import PartitionSpec as P

HEADS = 12
HEAD = 128
KV_HEADS = 2
RESP = 32
CACHE = 384


def span_mask(lengths, sink_count, window_size):
    cache_pos = jnp.arange(CACHE, dtype=jnp.int32)
    slot_pos = jnp.arange(RESP, dtype=jnp.int32)
    req_count = lengths.shape[0]
    key_pos = jnp.concatenate([cache_pos[None, :], lengths[:, None] + slot_pos[None, :]], axis=1)
    key_live = jnp.concatenate(
        [cache_pos[None, :] < lengths[:, None], jnp.ones((req_count, RESP), jnp.bool_)], axis=1
    )
    query_pos = lengths[:, None] + slot_pos[None, :]
    earlier = key_pos[:, None, :] <= query_pos[:, :, None]
    inside = (key_pos[:, None, :] < sink_count[0]) | (
        query_pos[:, :, None] - key_pos[:, None, :] < window_size[0]
    )
    return key_live[:, None, :] & earlier & inside


def rms_norm(hidden, norm_gain):
    scale_inv = lax.rsqrt(jnp.mean(hidden * hidden, axis=-1, keepdims=True) + 1e-06)
    return (hidden * scale_inv * norm_gain[:, None, None, :]).astype(jnp.bfloat16)


def per_device(
    queries,
    response_kv,
    cache_kv,
    residual,
    out_proj,
    norm_gain,
    lm_head,
    targets,
    resp_lengths,
    cache_lengths,
    owner_slot,
    sink_count,
    window_size,
):
    tp_size = lax.axis_size("tp")
    tp_index = lax.axis_index("tp")
    req_index = lax.axis_index("req")
    local_reqs = queries.shape[1]
    local_heads = HEADS // tp_size
    group_size = HEADS // KV_HEADS
    kv_index = tp_index * local_heads // group_size
    quarter = RESP // tp_size
    cache_head = lax.dynamic_slice_in_dim(cache_kv, kv_index * HEAD, HEAD, axis=4)
    resp_head = lax.dynamic_slice_in_dim(response_kv, kv_index * HEAD, HEAD, axis=4)
    key_rows = jnp.concatenate([cache_head[:, :, 0], resp_head[:, :, 0]], axis=2)
    value_rows = jnp.concatenate([cache_head[:, :, 1], resp_head[:, :, 1]], axis=2)
    query_heads = queries.reshape(2, local_reqs, RESP, local_heads, HEAD)
    scores = jnp.einsum(
        "mrshd,mrkd->mrhsk", query_heads, key_rows, preferred_element_type=jnp.float32
    ) * HEAD ** (-0.5)
    allowed = span_mask(cache_lengths, sink_count, window_size)[None, :, None]
    masked = jnp.where(allowed, scores, -jnp.inf)
    row_peak = jnp.max(masked, axis=-1, keepdims=True)
    weights = jnp.exp(masked - row_peak)
    weights = (weights / jnp.sum(weights, axis=-1, keepdims=True)).astype(jnp.bfloat16)
    attended = jnp.einsum(
        "mrhsk,mrkd->mrshd", weights, value_rows, preferred_element_type=jnp.float32
    )
    attended = attended.astype(jnp.bfloat16).reshape(2, local_reqs, RESP, local_heads * HEAD)
    partial_value = jnp.einsum(
        "mrsf,mfd->mrsd", attended, out_proj, preferred_element_type=jnp.float32
    )
    start_slot = tp_index * quarter
    projected = lax.dynamic_slice_in_dim(lax.psum(partial_value, "tp"), start_slot, quarter, axis=2)
    own_residual = lax.dynamic_slice_in_dim(residual, start_slot, quarter, axis=2)
    hidden = own_residual.astype(jnp.float32) + projected
    normed = rms_norm(hidden, norm_gain)
    flat_rows = normed.reshape(2, local_reqs * quarter, normed.shape[3])
    full_head = lax.all_gather(lm_head, "tp", axis=2, tiled=True)
    vocab_rows = full_head.shape[1]
    vocab_start = req_index * vocab_rows
    flat_targets = targets.reshape(-1)
    total_rows = flat_targets.shape[0]
    requests = total_rows // quarter
    logits = jnp.einsum(
        "mnd,mvd->mnv",
        lax.all_gather(flat_rows, "req", axis=1, tiled=True),
        full_head,
        preferred_element_type=jnp.float32,
    )
    block_peak = jnp.max(logits, axis=-1)
    block_total = jnp.sum(jnp.exp(logits - block_peak[..., None]), axis=-1)
    wanted = flat_targets - vocab_start
    target_hits = jnp.arange(vocab_rows, dtype=jnp.int32)[None, None, :] == wanted[None, :, None]
    block_pick = jnp.sum(jnp.where(target_hits, logits, 0.0), axis=-1)
    peak_all = block_peak
    total_all = block_total
    picked_all = block_pick
    peak_all = peak_all.reshape(2, requests, quarter)
    total_all = total_all.reshape(2, requests, quarter)
    picked_all = picked_all.reshape(2, requests, quarter)
    row_order = (
        jnp.zeros((requests,), jnp.int32).at[owner_slot].set(jnp.arange(requests, dtype=jnp.int32))
    )
    owned_reqs = lax.dynamic_slice_in_dim(row_order, req_index * local_reqs, local_reqs)
    vocab_top = lax.pmax(peak_all, "req")
    exp_total, picked = lax.psum((total_all * jnp.exp(peak_all - vocab_top), picked_all), "req")
    logprob = (picked - (vocab_top + jnp.log(exp_total)))[:, owned_reqs]
    lengths_owned = resp_lengths[owned_reqs]
    live_slots = (start_slot + jnp.arange(quarter, dtype=jnp.int32))[None, :] < lengths_owned[
        :, None
    ]
    policy = jnp.where(live_slots, logprob[0], 0.0)
    log_ratio = jnp.where(live_slots, logprob[0] - logprob[1], 0.0)
    policy_total, ratio_total = lax.psum(
        (jnp.sum(policy, axis=1), jnp.sum(log_ratio, axis=1)), "tp"
    )
    counts = lengths_owned.astype(jnp.float32)
    request_scores = jnp.stack([policy_total / counts, ratio_total / counts], axis=1)
    return (policy, request_scores)


def solution(mesh):
    in_specs = (
        P(None, "req", None, "tp"),
        P(None, "req", None, None, None),
        P(None, "req", None, None, None),
        P(None, "req", None, None),
        P(None, "tp", None),
        P(),
        P(None, "req", "tp"),
        P(None, "tp"),
        P(),
        P("req"),
        P(),
        P(),
        P(),
    )
    out_specs = (P("req", "tp"), P("req", None))
    return jax.shard_map(
        per_device, mesh=mesh, in_specs=in_specs, out_specs=out_specs, check_vma=False
    )
```

profile of v0, /device:TPU:8, one launch (start us, length us, event | category | flops | bytes accessed | tf_op | source)
XLA Modules:
  0.0 1325.8 jit_solution(16412632593061100903)
XLA Ops:
  7.2 0.0 copy-start
  7.2 0.0 copy-start.1
  7.2 0.0 copy-start.2
  7.2 0.0 copy-start.3
  7.2 0.0 copy-start.4
  7.2 0.0 copy-start.5
  7.2 0.0 all-reduce.5.cloned.1.call-start
  7.3 1.2 dynamic-slice_bitcast_fusion
  8.5 0.8 dynamic-slice_bitcast_fusion.2
  11.3 0.8 reshape.303
  12.1 0.1 fusion.12
  12.2 0.3 fusion.23
  12.6 0.2 fusion.5
  12.8 0.3 fusion.4
  13.1 0.1 reshape.305
  13.2 0.0 copy-done
  13.2 1.3 convolution_bitcast_fusion
  14.4 0.0 all-reduce.5.cloned.1.call-update
  14.4 0.0 all-gather.4.cloned.1.call-start
  14.5 0.7 all-gather.4.cloned.1.call-update
  15.2 0.0 all-gather.6.cloned.1.call-start
  15.3 60.6 %all-reduce.5.cloned.1.call-done = f32[2,1,32,1536]{3,2,0,1:T(8,128)} async-done(((f32[2,1,32,1536]{3,2,0,1:T(8,128)}), f32[2,1,32,1536]{3,2,0,1:T(8,128)}) %all-reduce.5.cloned.1.call-update) | async-done | bytes 393232 | tf_op jit(solution)/shard_map/psum | solution.py:78
  75.8 0.0 copy-done.1
  75.8 1.0 multiply_reduce_fusion
  76.8 0.0 copy-done.2
  76.9 1.6 multiply_convert_fusion
  78.4 0.0 all-gather.6.cloned.1.call-update
  78.5 0.0 copy-done.3
  78.5 0.1 copy.19
  78.6 0.1 sub.65
  78.7 1.0 scatter_custom_fusion
  79.7 0.6 dynamic_slice.15
  82.2 0.0 copy-done.5
  82.2 0.6 dynamic-slice.5
  83.5 0.8 iota_compare_fusion
  84.3 68.4 %all-gather.4.cloned.1.call-done = bf16[2,1024,1536]{2,1,0:T(8,128)(2,1)} async-done(((bf16[2,1024,384]{2,1,0:T(8,128)(2,1)}), bf16[2,1024,1536]{2,1,0:T(8,128)(2,1)}) %all-gather.4.cloned.1.call-update) | async-done | bytes 6291472 | tf_op jit(solution)/shard_map/all_gather | solution.py:83
  152.7 149.5 %all-gather.6.cloned.1.call-done = bf16[2,1,1024,1536]{3,2,0,1:T(8,128)(2,1)} async-done(((bf16[2,1,8,1536]{3,2,0,1:T(8,128)(2,1)}), bf16[2,1,1024,1536]{3,2,0,1:T(8,128)(2,1)}) %all-gather.6.cloned.1.call-update) | async-done | bytes 6291472 | tf_op jit(solution)/shard_map/all_gather | solution.py:91
  302.2 12.7 fusion.24
  314.9 0.1 reshape.308
  315.0 5.1 exponential_reduce_fusion
  320.1 0.8 reshape.309
  320.9 493.2 %pmax.7 = f32[2,128,8]{2,1,0:T(8,128)S(1)} all-reduce(f32[2,128,8]{2,1,0:T(8,128)S(1)} %reshape.308), channel_id=1, replica_groups=mesh['req'=128,'tp'=4] {'req'}, use_global_device_ids=true, to_apply=%region_8.9 | all-reduce | flops 2048 | bytes 16384 | tf_op jit(solution)/shard_map/pmax | solution.py:110
  814.1 0.1 reshape.307
  814.2 490.9 %all-reduce.1 = (f32[2,128,8]{2,1,0:T(8,128)S(1)}, f32[2,128,8]{2,1,0:T(8,128)S(1)}) all-reduce(f32[2,128,8]{2,1,0:T(8,128)S(1)} %reshape.307, f32[2,128,8]{2,1,0:T(8,128)S(1)} %exponential_multiply_fusion), channel_id=1, replica_groups=mesh['req'=128,'tp'=4] {'req'}, use_global_device_ids=true, to_apply=%region_6.7 | all-reduce | flops 4096 | bytes 32768 | tf_op jit(solution)/shard_map/psum | solution.py:111
  1305.2 1.2 fusion.17
  1306.4 1.7 fusion.22
  1308.1 9.3 all-reduce.2
  1318.7 0.6 pad_maximum_fusion
  (15 shorter events, 0.2 us)
Async XLA Ops:
  7.2 6.0 copy-start
  7.2 68.7 %copy-start.1 = (bf16[2,1,32,1536]{3,2,1,0:T(8,128)(2,1)S(1)}, bf16[2,1,32,1536]{3,2,1,0:T(8,128)(2,1)}, u32[]{:S(2)}) copy-start(bf16[2,1,32,1536]{3,2,1,0:T(8,128)(2,1)} %param.16) | copy-start | bytes 589828
  7.2 69.7 %copy-start.2 = (f32[2,1536]{1,0:T(2,128)S(1)}, f32[2,1536]{1,0:T(2,128)}, u32[]{:S(2)}) copy-start(f32[2,1536]{1,0:T(2,128)} %param.18) | copy-start | bytes 36868
  7.2 71.3 %copy-start.3 = (s32[128,8]{0,1:T(8,128)S(1)}, s32[128,8]{0,1:T(8,128)}, u32[]{:S(2)}) copy-start(s32[128,8]{0,1:T(8,128)} %param.20) | copy-start | bytes 12292
  7.2 71.5 %copy-start.4 = (s32[128]{0:T(128)S(1)}, s32[128]{0:T(128)}, u32[]{:S(2)}) copy-start(s32[128]{0:T(128)} %param.23) | copy-start | bytes 1540
  7.2 75.0 %copy-start.5 = (s32[128]{0:T(128)S(1)}, s32[128]{0:T(128)}, u32[]{:S(2)}) copy-start(s32[128]{0:T(128)} %param.21) | copy-start | bytes 1540
  7.2 68.6 %all-reduce.5.cloned.1.call-start = ((), (), s32[]{:S(2)}) async-start(), calls=%async_computation | async-start | bytes 786432 | tf_op jit(solution)/shard_map/psum | solution.py:78
  14.4 138.2 %all-gather.4.cloned.1.call-start = ((), (), s32[]{:S(2)}) async-start(), calls=%async_computation.1 | async-start | bytes 7864320 | tf_op jit(solution)/shard_map/all_gather | solution.py:83
  15.2 287.0 %all-gather.6.cloned.1.call-start = ((), (), s32[]{:S(2)}) async-start(), calls=%async_computation.2 | async-start | bytes 6340608 | tf_op jit(solution)/shard_map/all_gather | solution.py:91
Sparse Core Ops, SparseCore 0:
  14.6 61.2 all-reduce.4
  78.2 74.4 all-gather.3
  156.4 145.7 all-gather.5
where the time goes:
time: 1330 us
  blocking collectives  993 us (75%)
  waiting for transfers between devices  279 us (21%)
  between operations  19.9 us (1%)
  matrix products  14.6 us (1%)
    pmax x1, blocking collectives, per_device(): vocab_top = lax.pmax(peak_all, 'req')  493 us
    psum x1, blocking collectives, per_device(): lax.psum((total_all * jnp.exp(peak_all - vocab_top), picked_all), 'req')  491 us
    all_gather x1, waiting for transfers between devices, per_device(): lax.all_gather(flat_rows, 'req', axis=1, tiled=True)  149 us
    all_gather x1, waiting for transfers between devices, per_device(): full_head = lax.all_gather(lm_head, 'tp', axis=2, tiled=True)  68.4 us
    psum x1, waiting for transfers between devices, per_device(): lax.psum(partial_value, 'tp')  60.6 us
  transfers between devices with their start and end apart: 3, of which 3 were waited for; matrix products, arithmetic and copies ran while one was open for 0% of the time, Pallas kernels for 0%

commit v1 on v0

--- a/solution.py
+++ b/solution.py
@@ -80,7 +80,19 @@
     hidden = own_residual.astype(jnp.float32) + projected
     normed = rms_norm(hidden, norm_gain)
     flat_rows = normed.reshape(2, local_reqs * quarter, normed.shape[3])
-    full_head = lax.all_gather(lm_head, "tp", axis=2, tiled=True)
+
+    def _settle_clusters(piece_in, bus_axis="tp"):
+        lanes = jax.lax.axis_size(bus_axis)
+        buffer = [piece_in]
+        for t in range(lanes - 1):
+            block_now = jax.lax.ppermute(
+                buffer[-1], bus_axis, [(num, (num + 1) % lanes) for num in range(lanes)]
+            )
+            buffer.append(block_now)
+        out_arr = jnp.concatenate(buffer[::-1], axis=2)
+        return jnp.roll(out_arr, (jax.lax.axis_index(bus_axis) + 1) * piece_in.shape[2], 2)
+
+    full_head = _settle_clusters(lm_head)
     vocab_rows = full_head.shape[1]
     vocab_start = req_index * vocab_rows
     flat_targets = targets.reshape(-1)

time: 1330 us -> 1250 us (0.940)
  waiting for transfers between devices: 279 us -> 172 us
  local copies, waits for them, and re-layouts: 6.31 us -> 25.5 us
    all_gather x1, waiting for transfers between devices: 149 us -> 20.8 us  [per_device(): lax.all_gather(flat_rows, 'req', axis=1, tiled=True)]
    ppermute x0 -> x3, waiting for transfers between devices: none -> 89.8 us  [_settle_clusters(): jax.lax.ppermute(buffer[-1], bus_axis, [(num, (num + 1) % lanes) for num...]
    all_gather x1 -> x0, waiting for transfers between devices: 68.4 us -> none  [per_device(): full_head = lax.all_gather(lm_head, 'tp', axis=2, tiled=True)]
    unnamed x12 -> x15, local copies, waits for them, and re-layouts: 0.03 us -> 17.2 us
  transfers between devices with their start and end apart: 3 -> 5, of which waited for: 3 -> 5; matrix products, arithmetic and copies ran while one was open for 0% -> 2% of each run, Pallas kernels for 0% -> 0%
where the time goes in v1:
time: 1250 us
  blocking collectives  993 us (79%)
  waiting for transfers between devices  172 us (14%)
  local copies, waits for them, and re-layouts  25.5 us (2%)
  between operations  20 us (2%)
  matrix products  14.7 us (1%)
  other arithmetic  13.7 us (1%)
    pmax x1, blocking collectives, per_device(): vocab_top = lax.pmax(peak_all, 'req')  493 us
    psum x1, blocking collectives, per_device(): lax.psum((total_all * jnp.exp(peak_all - vocab_top), picked_all), 'req')  491 us
    ppermute x3, waiting for transfers between devices, _settle_clusters(): jax.lax.ppermute(buffer[-1], bus_axis, [(num, (num + 1) % lanes) for num...  89.8 us
    psum x1, waiting for transfers between devices, per_device(): lax.psum(partial_value, 'tp')  61.3 us
  transfers between devices with their start and end apart: 5, of which 5 were waited for; matrix products, arithmetic and copies ran while one was open for 2% of the time, Pallas kernels for 0%

profile of v1, /device:TPU:8, one launch (start us, length us, event | category | flops | bytes accessed | tf_op | source)
XLA Modules:
  0.0 1249.5 jit_solution(1877286049161735090)
XLA Ops:
  7.3 0.9 dynamic-slice_bitcast_fusion.2
  8.2 1.0 dynamic-slice_bitcast_fusion
  9.2 0.8 reshape.303
  12.1 0.1 fusion.13
  12.2 0.3 fusion.25
  12.5 0.2 fusion.6
  12.7 0.3 fusion.5
  13.0 0.1 reshape.305
  13.1 1.3 convolution_bitcast_fusion
  14.4 0.0 all-gather.3.cloned.1.call-start
  14.4 61.3 %all-reduce.5.cloned.1.call-done = f32[2,1,32,1536]{3,2,0,1:T(8,128)} async-done(((f32[2,1,32,1536]{3,2,0,1:T(8,128)}), f32[2,1,32,1536]{3,2,0,1:T(8,128)}) %all-reduce.5.cloned.1.call-update) | async-done | bytes 393232 | tf_op jit(solution)/shard_map/psum | solution.py:78
  75.8 1.0 multiply_reduce_fusion
  76.8 1.6 multiply_convert_fusion
  78.4 3.5 collective-permute-start
  81.9 32.7 %collective-permute-done = bf16[2,1024,384]{2,1,0:T(8,128)(2,1)S(1)} collective-permute-done((bf16[2,1024,384]{2,1,0:T(8,128)(2,1)}, bf16[2,1024,384]{2,1,0:T(8,128)(2,1)S(1)}, u32[]{:S(2)}, u32[]{:S(2)}) %collective-permute-start) | collective-permute-done | bytes 1572896 | tf_op jit(solution)/shard_map/ppermute | solution.py:88
  114.6 1.1 copy-done.2
  115.7 3.6 collective-permute-start.1
  119.3 32.3 %collective-permute-done.1 = bf16[2,1024,384]{2,1,0:T(8,128)(2,1)} collective-permute-done((bf16[2,1024,384]{2,1,0:T(8,128)(2,1)S(1)}, bf16[2,1024,384]{2,1,0:T(8,128)(2,1)}, u32[]{:S(2)}, u32[]{:S(2)}) %collective-permute-start.1) | collective-permute-done | bytes 1572896 | tf_op jit(solution)/shard_map/ppermute | solution.py:88
  151.6 3.0 collective-permute-start.2
  154.6 0.7 broadcast_subtract_fusion
  155.3 0.1 copy.19
  155.4 0.1 sub.69
  155.5 0.7 compare_select_fusion
  156.2 1.0 scatter_custom_fusion
  157.1 0.6 dynamic_slice.19
  159.7 1.2 dynamic-slice.5
  161.5 0.8 iota_compare_fusion
  162.3 24.9 %collective-permute-done.2 = bf16[2,1024,384]{2,1,0:T(8,128)(2,1)} collective-permute-done((bf16[2,1024,384]{2,1,0:T(8,128)(2,1)}, bf16[2,1024,384]{2,1,0:T(8,128)(2,1)}, u32[]{:S(2)}, u32[]{:S(2)}) %collective-permute-start.2) | collective-permute-done | bytes 1572896 | tf_op jit(solution)/shard_map/ppermute | solution.py:88
  187.2 3.0 constant_dynamic-update-slice_fusion.7
  190.2 2.8 constant_dynamic-update-slice_fusion.6
  193.0 1.4 constant_dynamic-update-slice_fusion.5
  194.5 1.5 constant_dynamic-update-slice_fusion.4
  196.0 2.8 constant_dynamic-update-slice_fusion.3
  198.8 2.9 constant_dynamic-update-slice_fusion.2
  201.7 1.5 constant_dynamic-update-slice_fusion.1
  203.2 1.5 constant_dynamic-update-slice_fusion
  204.7 20.8 %all-gather.3.cloned.1.call-done = bf16[2,1,1024,1536]{3,2,0,1:T(8,128)(2,1)} async-done(((bf16[2,1,8,1536]{3,2,0,1:T(8,128)(2,1)}), bf16[2,1,1024,1536]{3,2,0,1:T(8,128)(2,1)}) %all-gather.3.cloned.1.call-update) | async-done | bytes 6291472 | tf_op jit(solution)/shard_map/all_gather | solution.py:103
  225.5 12.9 %fusion.26 = (f32[2,1024]{1,0:T(2,128)S(1)}, f32[2,1024,1024]{1,2,0:T(8,128)}) fusion(bf16[2,1024,3072]{2,1,0:T(8,128)(2,1)} %constant_dynamic-update-slice_fusion, s32[]{:T(128)S(6)} %select_n.69, bf16[2,1,1024,1536]{3,2,0,1:T(8,128)(2,1)} %all-gather.3.cloned.1.call-done), kind=kOutput, calls=%fused_computation.70 | convolution fusion | flops 6444546048 | bytes 20979716 | tf_op jit(solution)/shard_map/mnd,mvd->mnv/dot_general | solution.py:101
  238.4 0.1 reshape.308
  238.5 5.1 exponential_reduce_fusion
  243.6 0.8 reshape.307
  244.4 0.1 reshape.309
  244.5 493.4 %pmax.7 = f32[2,128,8]{2,1,0:T(8,128)S(1)} all-reduce(f32[2,128,8]{2,1,0:T(8,128)S(1)} %reshape.308), channel_id=1, replica_groups=mesh['req'=128,'tp'=4] {'req'}, use_global_device_ids=true, to_apply=%region_8.9 | all-reduce | flops 2048 | bytes 16384 | tf_op jit(solution)/shard_map/pmax | solution.py:122
  737.9 490.9 %all-reduce.1 = (f32[2,128,8]{2,1,0:T(8,128)S(1)}, f32[2,128,8]{2,1,0:T(8,128)S(1)}) all-reduce(f32[2,128,8]{2,1,0:T(8,128)S(1)} %reshape.307, f32[2,128,8]{2,1,0:T(8,128)S(1)} %exponential_multiply_fusion), channel_id=1, replica_groups=mesh['req'=128,'tp'=4] {'req'}, use_global_device_ids=true, to_apply=%region_6.7 | all-reduce | flops 4096 | bytes 32768 | tf_op jit(solution)/shard_map/psum | solution.py:123
  1228.8 1.7 fusion.24
  1230.5 1.2 fusion.19
  1231.7 9.1 all-reduce.2
  1242.0 0.6 pad_maximum_fusion
  (22 shorter events, 0.2 us)
Async XLA Ops:
  7.2 5.9 copy-start
  7.2 68.6 %all-reduce.5.cloned.1.call-start = ((), (), s32[]{:S(2)}) async-start(), calls=%async_computation | async-start | bytes 786432 | tf_op jit(solution)/shard_map/psum | solution.py:78
  14.4 211.1 %all-gather.3.cloned.1.call-start = ((), (), s32[]{:S(2)}) async-start(), calls=%async_computation.1 | async-start | bytes 6340608 | tf_op jit(solution)/shard_map/all_gather | solution.py:103
  78.4 36.1 %collective-permute-start = (bf16[2,1024,384]{2,1,0:T(8,128)(2,1)}, bf16[2,1024,384]{2,1,0:T(8,128)(2,1)S(1)}, u32[]{:S(2)}, u32[]{:S(2)}) collective-permute-start(bf16[2,1024,384]{2,1,0:T(8,128)(2,1)} %param.19), channel_id=1, source_target_pairs={{0,1},{1,2},{2,3},{3,0},{4,5},{5,6},{6,7},{7,4},{8,9},{9,10},{10,1... | collective-permute-start | bytes 4718600 | tf_op jit(solution)/shard_map/ppermute | solution.py:88
  114.6 1.1 copy-start.2
  115.7 35.9 %collective-permute-start.1 = (bf16[2,1024,384]{2,1,0:T(8,128)(2,1)S(1)}, bf16[2,1024,384]{2,1,0:T(8,128)(2,1)}, u32[]{:S(2)}, u32[]{:S(2)}) collective-permute-start(bf16[2,1024,384]{2,1,0:T(8,128)(2,1)S(1)} %collective-permute-done), channel_id=1, source_target_pairs={{0,1},{1,2},{2,3},{3,0},{4,5},{5,6},{6,7},{7,4},{8,9},{9,10},{10,1... | collective-permute-start | bytes 4718600 | tf_op jit(solution)/shard_map/ppermute | solution.py:88
  151.6 35.6 %collective-permute-start.2 = (bf16[2,1024,384]{2,1,0:T(8,128)(2,1)}, bf16[2,1024,384]{2,1,0:T(8,128)(2,1)}, u32[]{:S(2)}, u32[]{:S(2)}) collective-permute-start(bf16[2,1024,384]{2,1,0:T(8,128)(2,1)} %collective-permute-done.1), channel_id=1, source_target_pairs={{0,1},{1,2},{2,3},{3,0},{4,5},{5,6},{6,7},{7,4},{8,9},{9,10},{10,1... | collective-permute-start | bytes 4718600 | tf_op jit(solution)/shard_map/ppermute | solution.py:88
  161.5 31.6 %copy-start.3 = (bf16[2,1024,384]{2,1,0:T(8,128)(2,1)S(1)}, bf16[2,1024,384]{2,1,0:T(8,128)(2,1)}, u32[]{:S(2)}) copy-start(bf16[2,1024,384]{2,1,0:T(8,128)(2,1)} %copy-done.2) | copy-start | bytes 4718596
  161.5 33.0 %copy-start.1 = (bf16[2,1024,384]{2,1,0:T(8,128)(2,1)S(1)}, bf16[2,1024,384]{2,1,0:T(8,128)(2,1)}, u32[]{:S(2)}) copy-start(bf16[2,1024,384]{2,1,0:T(8,128)(2,1)} %param.19) | copy-start | bytes 4718596
Sparse Core Ops, SparseCore 0:
  14.5 61.2 all-reduce.4
  79.4 145.9 all-gather.2
